TPU v7x, 128 devices: a whole 4x4x4 slice. The times are simulated.
128 devices in a mesh: sta: 64 (over x, y, z_hi, core), per: 2 (over z_lo).
Axes of the slice: x: 4, y: 4, z: 4 (z_hi: 2, z_lo: 2; z = z_hi * 2 + z_lo), core: 2. Of those that a mesh axis runs over, the one named last changes fastest.
Arguments:
- spectra: bfloat16 [1024, 2, 8192], P('sta', None, 'per'), may hold values from -6 to 6
- pick_bins: int32 [8, 1024, 48], P(None, ('sta', 'per')), may hold values from 0 to 127
- path_cells: int32 [1024, 2, 48], P(('sta', 'per')), may hold values from 0 to 8191
Outputs:
- helmholtz: float32 [8, 64, 128], P('per', 'sta')
All inputs are finite; a program needn't handle non-finite values.
Results may differ from a plain program's by a relative error of at most 0.0042.
Values may be sent and summed in bfloat16 or wider, within the bound.
A program may use at most 64 MiB of HBM per device.

v0:
```python
import math

import jax
import jax.numpy as jnp
from jax import lax
from jax.sharding import PartitionSpec as P

FREQ = 8192
NLAG = 128
ROWS_DEV = 1
MAP_COLS = 128


def passed_along(value, axis, by):
    peers = lax.axis_size(axis)
    return lax.ppermute(value, axis, [(i, (i + by) % peers) for i in range(peers)])


def padded_2(cells, sides, width):
    for axis, dim in sides:
        count = lax.axis_size(axis)
        ends = count - 1
        head = lax.slice_in_dim(cells, 0, width, axis=dim)
        tail = lax.slice_in_dim(cells, cells.shape[dim] - width, cells.shape[dim], axis=dim)
        cells = jnp.concatenate(
            [
                lax.ppermute(tail, axis, [(i, (i + 1) % count) for i in range(ends)]),
                cells,
                lax.ppermute(head, axis, [((i + 1) % count, i) for i in range(ends)]),
            ],
            axis=dim,
        )
    return cells


def lag_table(first_bin, bin_count, lag_count, total_bins):
    freq_index = (first_bin + jnp.arange(bin_count, dtype=jnp.int32))[:, None]
    lag_index = jnp.arange(lag_count, dtype=jnp.int32)[None, :] - lag_count // 2
    turned = freq_index * lag_index % (2 * total_bins)
    phase = turned.astype(jnp.float32) * (math.pi / total_bins)
    scale = total_bins ** (-0.5)
    return jnp.stack([jnp.cos(phase) * scale, -jnp.sin(phase) * scale]).astype(jnp.bfloat16)


def cross_block(resident, visiting, table_part):
    resident_re = resident[:, 0].astype(jnp.float32)[:, None, :]
    resident_im = resident[:, 1].astype(jnp.float32)[:, None, :]
    visiting_re = visiting[:, 0].astype(jnp.float32)[None, :, :]
    visiting_im = visiting[:, 1].astype(jnp.float32)[None, :, :]
    cross_re = (resident_re * visiting_re + resident_im * visiting_im).astype(jnp.bfloat16)
    cross_im = (resident_im * visiting_re - resident_re * visiting_im).astype(jnp.bfloat16)
    stacked = jnp.stack([cross_re, cross_im], axis=2)
    pair_rows = stacked.shape[0] * stacked.shape[1]
    return jnp.dot(
        stacked.reshape(pair_rows, -1),
        table_part.reshape(-1, table_part.shape[-1]),
        preferred_element_type=jnp.float32,
    )


def correlate(resident, visitors, cos_table):
    res_count = resident.shape[0]
    vis_count = visitors[0].shape[0]
    lag_count = cos_table.shape[2]
    block_width = resident.shape[2] // 16

    def add_block(block_index, totals):
        first_bin = block_index * block_width
        table_part = lax.dynamic_slice_in_dim(cos_table, first_bin, block_width, 1)
        resident_part = lax.dynamic_slice_in_dim(resident, first_bin, block_width, 2)
        updated = []
        for number, visitor in enumerate(visitors):
            visitor_part = lax.dynamic_slice_in_dim(visitor, first_bin, block_width, 2)
            updated.append(totals[number] + cross_block(resident_part, visitor_part, table_part))
        return tuple(updated)

    initial = tuple(
        (jnp.zeros((res_count * vis_count, lag_count), jnp.float32) for visitor in visitors)
    )
    totals = lax.fori_loop(0, 16, add_block, initial)
    panels = [total.reshape(res_count, vis_count, lag_count) for total in totals]
    res_global = jnp.arange(res_count, dtype=jnp.int32)
    not_self = (res_global[:, None] != jnp.arange(vis_count, dtype=jnp.int32)[None, :]).astype(
        jnp.float32
    )
    panels[0] = panels[0] * not_self[:, :, None]
    return jnp.stack(panels, axis=1)


def pick_lags(correlations, bins):
    row_count = correlations.shape[0]
    pair_cols = correlations.shape[1] * correlations.shape[2]
    flat = correlations.reshape(row_count, pair_cols, correlations.shape[3])
    chosen = jnp.take_along_axis(flat, jnp.transpose(bins, (1, 2, 0)), axis=2)
    return jnp.transpose(chosen, (2, 0, 1))


def visit_blocks(source):
    visitors = []
    current = source
    for repeat in range(2):
        current = passed_along(current, "sta", 1)
        visitors.append(current)
    return (visitors[0], visitors[1])


def on_device(spectra, pick_bins, path_cells):
    per_count = lax.axis_size("per")
    sta_count = lax.axis_size("sta")
    per_place = lax.axis_index("per")
    block_rows = spectra.shape[0]
    band = spectra.shape[2]
    half_rows = block_rows // per_count
    cos_table = lag_table(per_place * band, band, NLAG, FREQ)
    near_visit, far_visit = visit_blocks(spectra)
    correlations = lax.psum_scatter(
        correlate(spectra, (spectra, near_visit, far_visit), cos_table),
        "per",
        scatter_dimension=0,
        tiled=True,
    )
    picked = pick_lags(correlations, pick_bins)
    periods = pick_bins.shape[0]
    pair_cols = picked.shape[2]
    spread = jnp.broadcast_to(picked[:, :, None, :], (periods, half_rows, 2, pair_cols)).reshape(
        periods, -1
    )
    deposits = jnp.stack([spread, spread * spread])
    flat_cells = path_cells.reshape(-1)
    row_len = ROWS_DEV * MAP_COLS
    block_of = flat_cells // row_len
    within = flat_cells % row_len
    map_grid = (
        jnp.zeros((2, periods, sta_count, row_len), jnp.float32)
        .at[:, :, block_of, within]
        .add(deposits)
    )
    map_grid = lax.psum_scatter(map_grid, "per", scatter_dimension=1, tiled=True)
    map_grid = lax.psum_scatter(map_grid, "sta", scatter_dimension=2, tiled=True)
    local_periods = periods // per_count
    padded = padded_2(map_grid, (("sta", 2),), 1)
    padded = jnp.pad(padded, ((0, 0), (0, 0), (0, 0), (1, 1)))
    field_u = padded[0]
    amplitude = 1.0 + padded[1]
    grad_rows = (field_u[:, 2:, 1:-1] - field_u[:, :-2, 1:-1]) * 0.5
    grad_cols = (field_u[:, 1:-1, 2:] - field_u[:, 1:-1, :-2]) * 0.5
    centre = amplitude[:, 1:-1, 1:-1]
    laplace = (
        amplitude[:, 2:, 1:-1]
        + amplitude[:, :-2, 1:-1]
        + amplitude[:, 1:-1, 2:]
        + amplitude[:, 1:-1, :-2]
        - 4.0 * centre
    )
    period_index = per_place * local_periods + jnp.arange(local_periods, dtype=jnp.int32)
    weight = 1.0 / (1.0 + period_index.astype(jnp.float32))
    return grad_rows * grad_rows + grad_cols * grad_cols - weight[:, None, None] * laplace / centre


def solution(mesh):
    return jax.shard_map(
        on_device,
        mesh=mesh,
        in_specs=(
            P("sta", None, "per"),
            P(None, ("sta", "per"), None),
            P(("sta", "per"), None, None),
        ),
        out_specs=P("per", "sta", None),
        check_vma=False,
    )
```

profile of v0, /device:TPU:0, one launch (start us, length us, event | category | flops | bytes accessed | tf_op | source)
XLA Modules:
  0.0 892.4 jit_solution(9034121873405660918)
XLA Ops:
  6.5 9.7 %multiply_convert_fusion.1 = (bf16[1,4096,128]{2,1,0:T(8,128)(2,1)S(1)}, bf16[1,4096,128]{2,1,0:T(8,128)(2,1)S(1)}) fusion(s32[128]{0:T(128)S(1)} %iota_add_fusion.1, s32[4096]{0:T(1024)S(1)} %iota_add_fusion), kind=kLoop, calls=%fused_computation.37 | loop fusion | flops 9961472 | bytes 2114048 | tf_op jit(solution)/shard_map/convert.8
  16.3 2.6 collective-permute-done
  22.0 8.4 collective-permute-done.1
  30.4 103.0 %while.18 = (s32[]{:T(128)}, f32[256,128]{1,0:T(8,128)S(1)}, f32[256,128]{1,0:T(8,128)S(1)}, f32[256,128]{1,0:T(8,128)S(1)}, bf16[16,2,4096]{2,1,0:T(2,128)(2,1)...) while((s32[]{:T(128)}, f32[256,128]{1,0:T(8,128)S(1)}, ...), condition=%wide.region_1.2_spmd.clone, body=%wide.region_0.1_spmd.clone.sunk | while | flops 104030216 | bytes 6602967 | solution.py:80
  31.5 1.7 add_convert_fusion.4
  37.9 1.7 add_convert_fusion.4
  44.3 1.7 add_convert_fusion.4
  50.8 1.7 add_convert_fusion.4
  57.2 1.7 add_convert_fusion.4
  63.7 1.7 add_convert_fusion.4
  76.6 1.7 add_convert_fusion.4
  83.0 1.7 add_convert_fusion.4
  89.4 1.7 add_convert_fusion.4
  95.8 1.7 add_convert_fusion.4
  108.7 1.7 add_convert_fusion.4
  134.8 11.2 %reduce-scatter.3.cloned.1.call-done = f32[8,3,16,128]{3,2,1,0:T(8,128)} async-done(((f32[16,3,16,128]{3,2,1,0:T(8,128)}), f32[8,3,16,128]{3,2,1,0:T(8,128)}) %reduce-scatter.3.cloned.1.call-update) | async-done | bytes 196624 | tf_op jit(solution)/shard_map/reduce_scatter | solution.py:116
  146.0 22.9 %gather_fusion = f32[3072]{0:T(1024)S(1)} fusion(f32[8,48,128]{2,1,0:T(8,128)} %bitcast.96, s32[3072]{0:T(1024)S(1)} %reshape.496), kind=kCustom, calls=%fused_computation | custom fusion | bytes 61440 | tf_op jit(solution)/shard_map/jit(take_along_axis)/gather | solution.py:94
  169.8 7.3 broadcast_in_dim.36
  177.1 73.3 %scatter_fusion = f32[2,8,64,128]{1,0,3,2:T(2,128)} fusion(f32[2,8,64,128]{1,0,3,2:T(2,128)} %broadcast_in_dim.36, s32[768]{0:T(1024)S(1)} %fusion.11, f32[768,2,8]{2,1,0:T(2,128)S(1)} %copy.45), kind=kCustom, calls=%fused_computation.1 | custom fusion | flops 12288 | bytes 153600 | tf_op jit(solution)/shard_map/scatter-add | solution.py:136
  250.4 7.7 copy.46
  258.2 18.5 %reduce-scatter.5.cloned.1.call-done = f32[2,4,64,128]{3,2,0,1:T(8,128)} async-done(((f32[2,8,64,128]{3,2,0,1:T(8,128)}), f32[2,4,64,128]{3,2,0,1:T(8,128)}) %reduce-scatter.5.cloned.1.call-update) | async-done | bytes 262160 | tf_op jit(solution)/shard_map/reduce_scatter | solution.py:138
  276.7 1.8 copy.47
  279.2 598.9 %all-reduce.4.cloned.1.call-done = f32[2,4,64,128]{3,1,0,2:T(4,128)} async-done(((f32[2,4,64,128]{3,1,0,2:T(4,128)}), f32[2,4,64,128]{3,1,0,2:T(4,128)}) %all-reduce.4.cloned.1.call-update) | async-done | bytes 262160
  880.7 3.0 collective-permute-start.2
  (323 shorter events, 92.4 us)
Async XLA Ops:
  6.5 139.5 %reduce-scatter.3.cloned.1.call-start = ((), (), s32[]{:S(2)}) async-start(), calls=%async_computation.2 | async-start | bytes 589824 | tf_op jit(solution)/shard_map/reduce_scatter | solution.py:116
  6.5 12.3 %collective-permute-start = (bf16[16,2,4096]{2,1,0:T(2,128)(2,1)}, bf16[16,2,4096]{2,1,0:T(2,128)(2,1)S(1)}, u32[]{:S(2)}, u32[]{:S(2)}) collective-permute-start(bf16[16,2,4096]{2,1,0:T(2,128)(2,1)} %param.5), channel_id=1, source_target_pairs={{0,2},{2,4},{4,6},{6,8},{8,10},{10,12},{12,14},{14,16},{16,18},{18... | collective-permute-start | bytes 786440 | tf_op jit(solution)/shard_map/ppermute | solution.py:16
  18.9 11.5 %collective-permute-start.1 = (bf16[16,2,4096]{2,1,0:T(2,128)(2,1)S(1)}, bf16[16,2,4096]{2,1,0:T(2,128)(2,1)S(1)}, u32[]{:S(2)}, u32[]{:S(2)}) collective-permute-start(bf16[16,2,4096]{2,1,0:T(2,128)(2,1)S(1)} %collective-permute-done), channel_id=1, source_target_pairs={{0,2},{2,4},{4,6},{6,8},{8,10},{10,12},{12,14},{14,16},{16,18},{18... | collective-permute-start | bytes 786440 | tf_op jit(solution)/shard_map/ppermute | solution.py:16
  30.4 103.9 %copy-start = (s32[8,8,48]{2,1,0:T(8,128)S(1)}, s32[8,8,48]{2,1,0:T(8,128)}, u32[]{:S(2)}) copy-start(s32[8,8,48]{2,1,0:T(8,128)} %param.6) | copy-start | bytes 36868
  30.4 104.2 %copy-start.1 = (s32[8,2,48]{2,1,0:T(2,128)S(1)}, s32[8,2,48]{2,1,0:T(2,128)}, u32[]{:S(2)}) copy-start(s32[8,2,48]{2,1,0:T(2,128)} %param.7) | copy-start | bytes 9220
  134.3 142.4 %reduce-scatter.5.cloned.1.call-start = ((), (), s32[]{:S(2)}) async-start(), calls=%async_computation.3 | async-start | bytes 786432 | tf_op jit(solution)/shard_map/reduce_scatter | solution.py:138
  250.4 28.2 %copy-start.2 = (u32[128]{0:T(128)S(1)}, u32[128]{0:T(128)}, u32[]{:S(2)}) copy-start(u32[128]{0:T(128)} %constant.156) | copy-start | bytes 1540
  258.1 620.0 %all-reduce.4.cloned.1.call-start = ((), (), s32[]{:S(2)}) async-start(), calls=%async_computation.4 | async-start | bytes 524288
  879.4 5.7 collective-permute-start.3
  880.7 4.4 collective-permute-start.2
Sparse Core Ops, SparseCore 0:
  134.4 11.5 reduce-scatter.2
  258.2 18.4 reduce-scatter.4
  279.2 598.8 all-reduce.3
where the time goes:
time: 897 us; the launch traced here: 892 us
  waiting for transfers between devices  640 us (71%)
  other arithmetic  159 us (18%)
  local copies, waits for them, and re-layouts  60.7 us (7%)
  between operations  13.3 us (1%)
  matrix products  10.9 us (1%)
    unnamed x4, waiting for transfers between devices  599 us
    scatter-add x1, other arithmetic, on_device(): map_grid = jnp.zeros((2, periods, sta_count, row_len), jnp.float32).at[:,...  73.3 us
    another operation x48, other arithmetic, cross_block(): stacked = jnp.stack([cross_re, cross_im], axis=2)  28.8 us
    convert_element_type x16, other arithmetic, cross_block(): (resident_re * visiting_re + resident_im * visiting_im).astype(jnp.bfloat16)  27.5 us
    gather x5, local copies, waits for them, and re-layouts, pick_lags(): chosen = jnp.take_along_axis(flat, jnp.transpose(bins, (1, 2, 0)), axis=2)  23.3 us
    reduce_scatter x1, waiting for transfers between devices, on_device(): lax.psum_scatter(map_grid, 'per', scatter_dimension=1, tiled=True)  18.5 us
  transfers between devices with their start and end apart: 7, of which 5 were waited for; matrix products, arithmetic and copies ran while one was open for 2% of the time, Pallas kernels for 0%

commit v1 on v0

v1 whole, which is shorter than its diff:
```python
import functools
import math

import jax
import jax.numpy as jnp
import numpy as np
from jax import lax
from jax.experimental import pallas as pl
from jax.experimental.pallas import tpu as pltpu
from jax.sharding import PartitionSpec as P

FREQ = 8192
NLAG = 128
COARSE = 128
MESH = pl.DeviceIdType.MESH


def angle_tables(per_count):
    lag = np.arange(NLAG, dtype=np.int64) - NLAG // 2
    coarse = np.arange(FREQ // COARSE, dtype=np.int64) * COARSE
    fine = np.arange(COARSE, dtype=np.int64)
    out = []
    for bins, scale in ((coarse, FREQ ** -0.5), (fine, 1.0)):
        turned = (bins[:, None] * lag[None, :]) % (2 * FREQ)
        phase = turned.astype(np.float64) * (math.pi / FREQ)
        out.append(np.stack([np.cos(phase), np.sin(phase)]).astype(np.float32) * np.float32(scale))
    coarse_table, fine_table = out
    coarse_table = coarse_table.reshape(2, per_count, -1, NLAG).transpose(1, 0, 2, 3)
    return coarse_table, fine_table


def build_table(coarse_ref, fine_ref, table_ref, per_place):
    band = table_ref.shape[1]

    def one(step, carry):
        c = coarse_ref[per_place, 0, pl.ds(step, 1), :]
        s = coarse_ref[per_place, 1, pl.ds(step, 1), :]
        rows = pl.ds(pl.multiple_of(step * COARSE, COARSE), COARSE)
        fc = fine_ref[0]
        fs = fine_ref[1]
        table_ref[0, rows, :] = (c * fc - s * fs).astype(jnp.bfloat16)
        table_ref[1, rows, :] = (-(s * fc + c * fs)).astype(jnp.bfloat16)
        return carry

    lax.fori_loop(0, band // COARSE, one, 0)


def correlate_into(acc_refs, res_ref, vis_refs, table_ref, chunk):
    count = res_ref.shape[1]
    band = res_ref.shape[2]
    for acc in acc_refs:
        acc[...] = jnp.zeros_like(acc)

    def one(step, carry):
        cols = pl.ds(pl.multiple_of(step * chunk, chunk), chunk)
        cos_part = table_ref[0, cols, :]
        sin_part = table_ref[1, cols, :]
        rre = res_ref[0, :, cols].astype(jnp.float32)
        rim = res_ref[1, :, cols].astype(jnp.float32)
        for acc, vis in zip(acc_refs, vis_refs):
            vre = vis[0, :, cols].astype(jnp.float32)
            vim = vis[1, :, cols].astype(jnp.float32)
            res, ims = [], []
            for i in range(count):
                a = rre[i:i + 1]
                b = rim[i:i + 1]
                res.append((a * vre + b * vim).astype(jnp.bfloat16))
                ims.append((b * vre - a * vim).astype(jnp.bfloat16))
            cre = jnp.concatenate(res, axis=0)
            cim = jnp.concatenate(ims, axis=0)
            acc[...] += jnp.dot(cre, cos_part, preferred_element_type=jnp.float32) + jnp.dot(
                cim, sin_part, preferred_element_type=jnp.float32
            )
        return carry

    lax.fori_loop(0, band // chunk, one, 0)


def own_kernel(res_ref, coarse_ref, fine_ref, table_ref, corr_ref):
    per_place = lax.axis_index("per")
    build_table(coarse_ref, fine_ref, table_ref, per_place)
    correlate_into([corr_ref], res_ref, [res_ref], table_ref, 512)


def visit_kernel(res_ref, near_ref, far_ref, table_ref, corr_ref, bins_ref, picks_ref, acc_near, acc_far):
    correlate_into([acc_near, acc_far], res_ref, [near_ref, far_ref], table_ref, 512)
    pairs = corr_ref.shape[0]
    periods = bins_ref.shape[0]
    half = periods // 2
    lag = lax.broadcasted_iota(jnp.int32, (NLAG, pairs), 0)
    for k, acc in enumerate((corr_ref, acc_near, acc_far)):
        turned = acc[...].T
        rows = []
        for p in range(periods):
            wanted = bins_ref[p:p + 1, k * pairs:(k + 1) * pairs]
            rows.append(jnp.sum(jnp.where(lag == wanted, turned, 0.0), axis=0, keepdims=True))
        got = jnp.concatenate(rows, axis=0)
        if k == 0:
            side = int(math.isqrt(pairs))
            place = lax.broadcasted_iota(jnp.int32, (periods, pairs), 1)
            got = jnp.where(place // side == place % side, 0.0, got)
        picks_ref[0, :, k * pairs:(k + 1) * pairs] = got[:half]
        picks_ref[1, :, k * pairs:(k + 1) * pairs] = got[half:]


def map_kernel(sta_count, picks_ref, cells_ref, out_ref, peer_picks, spread, landed, edge_own, edges,
               lhs, pick_sems, send_sem, recv_sem, edge_send, edge_recv):
    sta = lax.axis_index("sta")
    per = lax.axis_index("per")
    others = sta_count - 1
    barrier = pltpu.get_barrier_semaphore()
    pl.semaphore_signal(barrier, inc=1, device_id=(sta, 1 - per), device_id_type=MESH)

    def greet(step, carry):
        there = lax.rem(sta + step, sta_count)
        pl.semaphore_signal(barrier, inc=1, device_id=(there, per), device_id_type=MESH)
        return carry

    lax.fori_loop(1, sta_count, greet, 0)
    pl.semaphore_wait(barrier, sta_count)

    trade = pltpu.make_async_remote_copy(
        src_ref=picks_ref.at[1 - per], dst_ref=peer_picks, send_sem=pick_sems.at[0], recv_sem=pick_sems.at[1],
        device_id=(sta, 1 - per), device_id_type=MESH)
    trade.start()
    cell = cells_ref[...]
    ends = cell.shape[1]
    col = cell % 128
    row = cell // 128
    col_hot = (lax.broadcasted_iota(jnp.int32, (128, ends), 0) == col).astype(jnp.bfloat16)
    trade.wait()
    total = picks_ref[per] + peer_picks[...]
    both = jnp.concatenate([total, total * total], axis=0)
    high = both.astype(jnp.bfloat16).astype(jnp.float32)
    low = both - high
    vals = jnp.concatenate([high, low], axis=0)
    vals = jnp.concatenate([vals, vals], axis=1)

    for r in range(sta_count):
        lhs[r * 16:(r + 1) * 16, :] = jnp.where(row == r, vals, 0.0).astype(jnp.bfloat16)
    grid = lax.dot_general(lhs[...], col_hot, (((1,), (1,)), ((), ())), preferred_element_type=jnp.float32)
    grid = grid.reshape(sta_count, 2, 8, 128)
    spread[...] = grid[:, 0] + grid[:, 1]

    def send(step, carry):
        there = lax.rem(sta + step, sta_count)
        pltpu.make_async_remote_copy(
            src_ref=spread.at[there], dst_ref=landed.at[step - 1], send_sem=send_sem, recv_sem=recv_sem,
            device_id=(there, per), device_id_type=MESH).start()
        return carry

    lax.fori_loop(1, sta_count, send, 0)
    pltpu.make_async_copy(landed, landed, recv_sem).wait()
    edge_own[...] = spread[sta] + jnp.sum(landed[...], axis=0)
    copies = []
    for side, step in enumerate((1, sta_count - 1)):
        there = lax.rem(sta + step, sta_count)
        copy = pltpu.make_async_remote_copy(
            src_ref=edge_own, dst_ref=edges.at[side], send_sem=edge_send.at[side], recv_sem=edge_recv.at[side],
            device_id=(there, per), device_id_type=MESH)
        copy.start()
        copies.append(copy)
    own = edge_own[...]
    half = own.shape[0] // 2
    lane = lax.broadcasted_iota(jnp.int32, own.shape, 1)
    before_col = jnp.where(lane == 0, 0.0, pltpu.roll(own, 1, 1))
    after_col = jnp.where(lane == 127, 0.0, pltpu.roll(own, 127, 1))
    for copy in copies:
        copy.wait()
    before = jnp.where(sta == 0, 0.0, edges[0])
    after = jnp.where(sta == sta_count - 1, 0.0, edges[1])
    grad_rows = (after[:half] - before[:half]) * 0.5
    grad_cols = (after_col[:half] - before_col[:half]) * 0.5
    amp = 1.0 + own[half:]
    laplace = ((1.0 + after[half:]) + (1.0 + before[half:]) + (1.0 + after_col[half:])
               + (1.0 + before_col[half:]) - 4.0 * amp)
    period = per * half + lax.broadcasted_iota(jnp.int32, laplace.shape, 0)
    weight = 1.0 / (1.0 + period.astype(jnp.float32))
    result = grad_rows * grad_rows + grad_cols * grad_cols - weight * laplace / amp
    out_ref[...] = result[:, None, :]
    pltpu.make_async_copy(landed, landed, send_sem).wait()


def on_device(spectra, pick_bins, path_cells):
    per_count = lax.axis_size("per")
    sta_count = lax.axis_size("sta")
    per_place = lax.axis_index("per")
    count, _, band = spectra.shape
    pairs = count * count
    periods = pick_bins.shape[0]
    offs = pick_bins.shape[2] // count
    parts = jnp.transpose(spectra, (1, 0, 2))

    def along(value, by):
        return lax.ppermute(value, "sta", [(i, (i + by) % sta_count) for i in range(sta_count)])

    near = along(parts, 1)
    far = along(parts, 2)
    swap = [(0, 1), (1, 0)]
    bins_other = lax.ppermute(pick_bins, "per", swap)
    cells_other = lax.ppermute(path_cells, "per", swap)
    first = per_place == 0
    bins = jnp.concatenate(
        [jnp.where(first, pick_bins, bins_other), jnp.where(first, bins_other, pick_bins)], axis=1)
    cells = jnp.concatenate(
        [jnp.where(first, path_cells, cells_other), jnp.where(first, cells_other, path_cells)], axis=0)
    bins = jnp.transpose(bins.reshape(periods, count, offs, count), (0, 2, 1, 3)).reshape(periods, -1)
    cells = jnp.transpose(cells.reshape(count, 2, offs, count), (1, 2, 0, 3)).reshape(1, -1)

    coarse, fine = angle_tables(per_count)
    vmem = pl.BlockSpec(memory_space=pltpu.VMEM)
    table, corr = pl.pallas_call(
        own_kernel,
        out_shape=(jax.ShapeDtypeStruct((2, band, NLAG), jnp.bfloat16),
                   jax.ShapeDtypeStruct((pairs, NLAG), jnp.float32)),
        in_specs=[vmem] * 3,
        out_specs=(vmem, vmem),
        cost_estimate=pl.CostEstimate(flops=2 * pairs * 2 * band * NLAG, bytes_accessed=4 << 20, transcendentals=0),
        name="own_block",
    )(parts, coarse, fine)
    picks = pl.pallas_call(
        visit_kernel,
        out_shape=jax.ShapeDtypeStruct((per_count, periods // 2, offs * pairs), jnp.float32),
        in_specs=[vmem] * 6,
        out_specs=vmem,
        scratch_shapes=[pltpu.VMEM((pairs, NLAG), jnp.float32)] * 2,
        cost_estimate=pl.CostEstimate(flops=4 * pairs * 2 * band * NLAG, bytes_accessed=4 << 20, transcendentals=0),
        name="visiting_blocks",
    )(parts, near, far, table, corr, bins)
    rows = 2 * periods // per_count
    return pl.pallas_call(
        functools.partial(map_kernel, sta_count),
        out_shape=jax.ShapeDtypeStruct((periods // per_count, 1, 128), jnp.float32),
        in_specs=[vmem] * 2,
        out_specs=vmem,
        scratch_shapes=[
            pltpu.VMEM((periods // 2, offs * pairs), jnp.float32),
            pltpu.VMEM((sta_count, rows, 128), jnp.float32),
            pltpu.VMEM((sta_count - 1, rows, 128), jnp.float32),
            pltpu.VMEM((rows, 128), jnp.float32),
            pltpu.VMEM((2, rows, 128), jnp.float32),
            pltpu.VMEM((sta_count * 2 * rows, 2 * offs * pairs), jnp.bfloat16),
            pltpu.SemaphoreType.DMA((2,)),
            pltpu.SemaphoreType.DMA,
            pltpu.SemaphoreType.DMA,
            pltpu.SemaphoreType.DMA((2,)),
            pltpu.SemaphoreType.DMA((2,)),
        ],
        compiler_params=pltpu.CompilerParams(collective_id=0, has_side_effects=True),
        name="map_exchange",
    )(picks, cells)


def solution(mesh):
    return jax.shard_map(
        on_device,
        mesh=mesh,
        in_specs=(
            P("sta", None, "per"),
            P(None, ("sta", "per"), None),
            P(("sta", "per"), None, None),
        ),
        out_specs=P("per", "sta", None),
        check_vma=False,
    )
```

time: 897 us -> 50.6 us (0.06)
  waiting for transfers between devices: 640 us -> 2.88 us
  other arithmetic: 159 us -> 0.03 us
  local copies, waits for them, and re-layouts: 60.7 us -> 4.75 us
  Pallas kernels: 0 us -> 36.4 us
  between operations: 13.3 us -> 0.09 us
  matrix products: 10.9 us -> 0 us
    unnamed x4 -> x0, waiting for transfers between devices: 599 us -> none
    scatter-add x1 -> x0, other arithmetic: 73.3 us -> none  [on_device(): map_grid = jnp.zeros((2, periods, sta_count, row_len), jnp.float32).at[:,...]
    another operation x52 -> x0, other arithmetic: 40.8 us -> none  [the longest x48 28.8 us: cross_block(): stacked = jnp.stack([cross_re, cross_im], axis=2)]
    pallas_call x0 -> x3, Pallas kernels: none -> 36.4 us  [the longest x1 24.5 us: on_device(): pl.pallas_call(functools.partial(map_kernel, sta_count), out_shape=jax.Sh...]
    reduce_scatter x2 -> x0, waiting for transfers between devices: 29.7 us -> none  [the longest x1 18.5 us: on_device(): lax.psum_scatter(map_grid, 'per', scatter_dimension=1, tiled=True)]
    convert_element_type x33 -> x0, other arithmetic: 29.6 us -> none  [the longest x16 27.5 us: cross_block(): (resident_re * visiting_re + resident_im * visiting_im).astype(jnp.bfloat16)]
    gather x5 -> x0, local copies, waits for them, and re-layouts: 23.3 us -> none  [pick_lags(): chosen = jnp.take_along_axis(flat, jnp.transpose(bins, (1, 2, 0)), axis=2)]
    dynamic_slice x16 -> x0, local copies, waits for them, and re-layouts: 14.8 us -> none  [add_block(): table_part = lax.dynamic_slice_in_dim(cos_table, first_bin, block_width, 1)]
  transfers between devices with their start and end apart: 7 -> 4, of which waited for: 5 -> 2; matrix products, arithmetic and copies ran while one was open for 2% -> 3% of each run, Pallas kernels for 0% -> 10%
where the time goes in v1:
time: 50.6 us; the launch traced here: 50.3 us
  Pallas kernels  36.4 us (72%)
  starting transfers between devices  6.16 us (12%)
  local copies, waits for them, and re-layouts  4.75 us (9%)
  waiting for transfers between devices  2.88 us (6%)
    pallas_call x1, Pallas kernels, on_device(): pl.pallas_call(functools.partial(map_kernel, sta_count), out_shape=jax.Sh...  24.5 us
    pallas_call x1, Pallas kernels, on_device(): pl.pallas_call(visit_kernel, out_shape=jax.ShapeDtypeStruct((per_count, p...  6.65 us
    pallas_call x1, Pallas kernels, on_device(): pl.pallas_call(own_kernel, out_shape=(jax.ShapeDtypeStruct((2, band, NLAG...  5.25 us
    ppermute x2, starting transfers between devices, along(): lax.ppermute(value, 'sta', [(i, (i + by) % sta_count) for i in range(sta_...  4.13 us
    unnamed x12, local copies, waits for them, and re-layouts  3.1 us
    ppermute x1, waiting for transfers between devices, on_device(): cells_other = lax.ppermute(path_cells, 'per', swap)  1.77 us
    ppermute x2, waiting for transfers between devices, along(): lax.ppermute(value, 'sta', [(i, (i + by) % sta_count) for i in range(sta_...  1.11 us
    ppermute x1, starting transfers between devices, on_device(): bins_other = lax.ppermute(pick_bins, 'per', swap)  1.02 us
  transfers between devices with their start and end apart: 4, of which 2 were waited for; matrix products, arithmetic and copies ran while one was open for 3% of the time, Pallas kernels for 10%

profile of v1, /device:TPU:0, one launch (start us, length us, event | category | flops | bytes accessed | tf_op | source)
XLA Modules:
  0.0 50.3 jit_solution(14266252599526441492)
XLA Ops:
  0.0 0.0 copy-start.1
  0.0 1.1 %copy.14 = bf16[16,2,4096]{2,0,1:T(8,128)(2,1)S(1)} copy(bf16[16,2,4096]{2,1,0:T(2,128)(2,1)} %param.5) | data formatting | bytes 524288 | tf_op args[0]
  1.1 0.0 copy-start
  1.1 0.1 collective-permute-start
  1.2 4.1 %collective-permute-start.1 = (bf16[2,16,4096]{2,1,0:T(8,128)(2,1)S(1)}, bf16[2,16,4096]{2,1,0:T(8,128)(2,1)S(1)}, u32[]{:S(2)}, u32[]{:S(2)}) collective-permute-start(bf16[2,16,4096]{2,1,0:T(8,128)(2,1)S(1)} %bitcast.18), channel_id=1, source_target_pairs={{0,4},{2,6},{4,8},{6,10},{8,12},{10,14},{12,16},{14,18},{16,20},{1... | collective-permute-start | bytes 786440 | tf_op jit(solution)/shard_map/ppermute | solution.py:195
  5.3 1.0 %collective-permute-start.2 = (s32[8,8,48]{2,1,0:T(8,128)}, s32[8,8,48]{2,1,0:T(8,128)S(1)}, u32[]{:S(2)}, u32[]{:S(2)}) collective-permute-start(s32[8,8,48]{2,1,0:T(8,128)} %param.6), channel_id=1, source_target_pairs={{0,1},{1,0},{2,3},{3,2},{4,5},{5,4},{6,7},{7,6},{8,9},{9,8},{10,11... | collective-permute-start | bytes 36872 | tf_op jit(solution)/shard_map/ppermute | solution.py:200
  6.3 1.0 %collective-permute-start.3 = (s32[8,2,48]{2,1,0:T(2,128)}, s32[8,2,48]{2,1,0:T(2,128)S(1)}, u32[]{:S(2)}, u32[]{:S(2)}) collective-permute-start(s32[8,2,48]{2,1,0:T(2,128)} %param.7), channel_id=1, source_target_pairs={{0,1},{1,0},{2,3},{3,2},{4,5},{5,4},{6,7},{7,6},{8,9},{9,8},{10,11... | collective-permute-start | bytes 9224 | tf_op jit(solution)/shard_map/ppermute | solution.py:201
  7.3 0.0 copy-done
  7.3 5.2 %own_block.1 = (bf16[2,4096,128]{2,1,0:T(8,128)(2,1)}, f32[256,128]{1,0:T(8,128)}) custom-call(bf16[2,16,4096]{2,1,0:T(8,128)(2,1)} %bitcast.19, f32[2,2,32,128]{3,2,1,0:T(8,128)} %constant.10.clone.coarse_ref, f32[2,128,128]{2,1,0:T(8,128)} %constant.11.clone.fine_ref), custom_call_target="tpu_custom_call" | custom-call | flops 536870912 | bytes 4194304 | tf_op jit(solution)/shard_map/own_block/pallas_call | solution.py:212
  12.6 1.8 %collective-permute-done.3 = s32[8,2,48]{2,1,0:T(2,128)S(1)} collective-permute-done((s32[8,2,48]{2,1,0:T(2,128)}, s32[8,2,48]{2,1,0:T(2,128)S(1)}, u32[]{:S(2)}, u32[]{:S(2)}) %collective-permute-start.3) | collective-permute-done | bytes 3104 | tf_op jit(solution)/shard_map/ppermute | solution.py:201
  14.3 0.0 copy-done.2
  14.4 0.1 reshape.14
  14.5 0.7 %reshape.15.cells_ref = s32[1,1536]{1,0:T(1,128)} reshape(s32[2,3,16,16]{3,2,1,0:T(8,128)S(1)} %copy.12) | data formatting | bytes 12288 | tf_op jit(solution)/shard_map/reshape | solution.py:208
  15.1 0.0 collective-permute-done.2
  15.1 0.0 copy-done.1
  15.2 0.1 reshape.12
  15.3 0.7 %reshape.13.bins_ref = s32[8,768]{1,0:T(8,128)} reshape(s32[8,3,16,16]{3,2,1,0:T(8,128)S(1)} %copy.10) | data formatting | bytes 49152 | tf_op jit(solution)/shard_map/reshape | solution.py:207
  16.1 0.0 collective-permute-done.near_ref
  16.1 1.1 %collective-permute-done.1.far_ref = bf16[2,16,4096]{2,1,0:T(8,128)(2,1)S(1)} collective-permute-done((bf16[2,16,4096]{2,1,0:T(8,128)(2,1)S(1)}, bf16[2,16,4096]{2,1,0:T(8,128)(2,1)S(1)}, u32[]{:S(2)}, u32[]{:S(2)}) %collective-permute-start.1) | collective-permute-done | bytes 262176 | tf_op jit(solution)/shard_map/ppermute | solution.py:195
  17.2 0.0 copy-done.3
  17.2 0.7 %copy-done.4 = bf16[2,16,4096]{2,1,0:T(8,128)(2,1)} copy-done((bf16[2,16,4096]{2,1,0:T(8,128)(2,1)}, bf16[2,16,4096]{2,1,0:T(8,128)(2,1)S(1)}, u32[]{:S(2)}) %copy-start.4) | copy-done | bytes 262168
  17.9 6.6 %visiting_blocks.1.picks_ref = f32[2,4,768]{2,1,0:T(4,128)} custom-call(bf16[2,16,4096]{2,1,0:T(8,128)(2,1)} %bitcast.20, bf16[2,16,4096]{2,1,0:T(8,128)(2,1)} %copy-done.3, bf16[2,16,4096]{2,1,0:T(8,128)(2,1)} %copy-done.4, bf16[2,4096,128]{2,1,0:T(8,128)(2,1)} %get-tuple-element.7.table_ref, f32[256,128]{1,0:T(8,128)} %get-tuple-element.8.corr_ref, ...), custom_call_target="tpu_custom_call" | custom-call | flops 1073741824 | bytes 4194304 | tf_op jit(solution)/shard_map/visiting_blocks/pallas_call | solution.py:221
  24.5 24.5 %map_exchange.1 = f32[4,1,128]{2,1,0:T(1,128)} custom-call(f32[2,4,768]{2,1,0:T(4,128)} %visiting_blocks.1.picks_ref, s32[1,1536]{1,0:T(1,128)} %reshape.15.cells_ref), custom_call_target="tpu_custom_call" | custom-call | tf_op jit(solution)/shard_map/map_exchange/pallas_call | solution.py:231
  49.1 1.3 %copy.16 = f32[4,1,128]{2,1,0:T(1,128)} copy(f32[4,1,128]{2,1,0:T(1,128)} %map_exchange.1) | data formatting | bytes 4096
  (10 shorter events, 0.1 us)
Async XLA Ops:
  0.0 15.1 %copy-start.1 = (s32[8,8,48]{2,1,0:T(8,128)S(1)}, s32[8,8,48]{2,1,0:T(8,128)}, u32[]{:S(2)}) copy-start(s32[8,8,48]{2,1,0:T(8,128)} %param.6) | copy-start | bytes 36868
  0.0 14.3 %copy-start.2 = (s32[8,2,48]{2,1,0:T(2,128)S(1)}, s32[8,2,48]{2,1,0:T(2,128)}, u32[]{:S(2)}) copy-start(s32[8,2,48]{2,1,0:T(2,128)} %param.7) | copy-start | bytes 9220
  1.1 6.2 %copy-start = (bf16[16,2,4096]{2,0,1:T(8,128)(2,1)}, bf16[16,2,4096]{2,0,1:T(8,128)(2,1)S(1)}, u32[]{:S(2)}) copy-start(bf16[16,2,4096]{2,0,1:T(8,128)(2,1)S(1)} %copy.14) | copy-start | bytes 786436
  1.1 14.9 %collective-permute-start = (bf16[2,16,4096]{2,1,0:T(8,128)(2,1)S(1)}, bf16[2,16,4096]{2,1,0:T(8,128)(2,1)S(1)}, u32[]{:S(2)}, u32[]{:S(2)}) collective-permute-start(bf16[2,16,4096]{2,1,0:T(8,128)(2,1)S(1)} %bitcast.17), channel_id=1, source_target_pairs={{0,2},{2,4},{4,6},{6,8},{8,10},{10,12},{12,14},{14,16},{16,18},{18... | collective-permute-start | bytes 786440 | tf_op jit(solution)/shard_map/ppermute | solution.py:195
  1.2 16.0 %collective-permute-start.1 = (bf16[2,16,4096]{2,1,0:T(8,128)(2,1)S(1)}, bf16[2,16,4096]{2,1,0:T(8,128)(2,1)S(1)}, u32[]{:S(2)}, u32[]{:S(2)}) collective-permute-start(bf16[2,16,4096]{2,1,0:T(8,128)(2,1)S(1)} %bitcast.18), channel_id=1, source_target_pairs={{0,4},{2,6},{4,8},{6,10},{8,12},{10,14},{12,16},{14,18},{16,20},{1... | collective-permute-start | bytes 786440 | tf_op jit(solution)/shard_map/ppermute | solution.py:195
  5.3 9.9 %collective-permute-start.2 = (s32[8,8,48]{2,1,0:T(8,128)}, s32[8,8,48]{2,1,0:T(8,128)S(1)}, u32[]{:S(2)}, u32[]{:S(2)}) collective-permute-start(s32[8,8,48]{2,1,0:T(8,128)} %param.6), channel_id=1, source_target_pairs={{0,1},{1,0},{2,3},{3,2},{4,5},{5,4},{6,7},{7,6},{8,9},{9,8},{10,11... | collective-permute-start | bytes 36872 | tf_op jit(solution)/shard_map/ppermute | solution.py:200
  6.3 8.0 %collective-permute-start.3 = (s32[8,2,48]{2,1,0:T(2,128)}, s32[8,2,48]{2,1,0:T(2,128)S(1)}, u32[]{:S(2)}, u32[]{:S(2)}) collective-permute-start(s32[8,2,48]{2,1,0:T(2,128)} %param.7), channel_id=1, source_target_pairs={{0,1},{1,0},{2,3},{3,2},{4,5},{5,4},{6,7},{7,6},{8,9},{9,8},{10,11... | collective-permute-start | bytes 9224 | tf_op jit(solution)/shard_map/ppermute | solution.py:201
  16.1 1.1 %copy-start.3 = (bf16[2,16,4096]{2,1,0:T(8,128)(2,1)}, bf16[2,16,4096]{2,1,0:T(8,128)(2,1)S(1)}, u32[]{:S(2)}) copy-start(bf16[2,16,4096]{2,1,0:T(8,128)(2,1)S(1)} %collective-permute-done.near_ref) | copy-start | bytes 786436
  17.2 0.7 %copy-start.4 = (bf16[2,16,4096]{2,1,0:T(8,128)(2,1)}, bf16[2,16,4096]{2,1,0:T(8,128)(2,1)S(1)}, u32[]{:S(2)}) copy-start(bf16[2,16,4096]{2,1,0:T(8,128)(2,1)S(1)} %collective-permute-done.1.far_ref) | copy-start | bytes 786436

commit v2 on v1

v2 whole, which is shorter than its diff:
```python
import functools
import math

import jax
import jax.numpy as jnp
import numpy as np
from jax import lax
from jax.experimental import pallas as pl
from jax.experimental.pallas import tpu as pltpu
from jax.sharding import PartitionSpec as P

FREQ = 8192
NLAG = 128
COARSE = 128
CHUNK = 512
MESH = pl.DeviceIdType.MESH


def angle_tables(per_count):
    lag = np.arange(NLAG, dtype=np.int64) - NLAG // 2
    coarse = np.arange(FREQ // COARSE, dtype=np.int64) * COARSE
    fine = np.arange(COARSE, dtype=np.int64)
    out = []
    for bins, scale in ((coarse, FREQ ** -0.5), (fine, 1.0)):
        turned = (bins[:, None] * lag[None, :]) % (2 * FREQ)
        phase = turned.astype(np.float64) * (math.pi / FREQ)
        out.append(np.stack([np.cos(phase), np.sin(phase)]).astype(np.float32) * np.float32(scale))
    coarse_table, fine_table = out
    coarse_table = coarse_table.reshape(2, per_count, -1, NLAG).transpose(1, 0, 2, 3)
    return coarse_table, fine_table


def build_table(coarse_ref, fine_ref, table_ref, per_place):
    band = table_ref.shape[1]

    def one(step, carry):
        c = coarse_ref[per_place, 0, pl.ds(step, 1), :]
        s = coarse_ref[per_place, 1, pl.ds(step, 1), :]
        rows = pl.ds(pl.multiple_of(step * COARSE, COARSE), COARSE)
        fc = fine_ref[0]
        fs = fine_ref[1]
        table_ref[0, rows, :] = (c * fc - s * fs).astype(jnp.bfloat16)
        table_ref[1, rows, :] = (-(s * fc + c * fs)).astype(jnp.bfloat16)
        return carry

    lax.fori_loop(0, band // COARSE, one, 0)


def correlate_into(acc_refs, res_ref, vis_refs, table_ref, chunk):
    count = res_ref.shape[1]
    band = res_ref.shape[2]
    for acc in acc_refs:
        acc[...] = jnp.zeros_like(acc)

    def one(step, carry):
        cols = pl.ds(pl.multiple_of(step * chunk, chunk), chunk)
        cos_part = table_ref[0, cols, :]
        sin_part = table_ref[1, cols, :]
        rre = res_ref[0, :, cols].astype(jnp.float32)
        rim = res_ref[1, :, cols].astype(jnp.float32)
        for acc, vis in zip(acc_refs, vis_refs):
            vre = vis[0, :, cols].astype(jnp.float32)
            vim = vis[1, :, cols].astype(jnp.float32)
            res, ims = [], []
            for i in range(count):
                a = rre[i:i + 1]
                b = rim[i:i + 1]
                res.append((a * vre + b * vim).astype(jnp.bfloat16))
                ims.append((b * vre - a * vim).astype(jnp.bfloat16))
            cre = jnp.concatenate(res, axis=0)
            cim = jnp.concatenate(ims, axis=0)
            acc[...] += jnp.dot(cre, cos_part, preferred_element_type=jnp.float32) + jnp.dot(
                cim, sin_part, preferred_element_type=jnp.float32
            )
        return carry

    lax.fori_loop(0, band // chunk, one, 0)


def take_picks(acc, bins, is_own):
    turned = acc.T
    periods, pairs = bins.shape
    lag = lax.broadcasted_iota(jnp.int32, turned.shape, 0)
    rows = []
    for p in range(periods):
        rows.append(jnp.sum(jnp.where(lag == bins[p:p + 1], turned, 0.0), axis=0, keepdims=True))
    got = jnp.concatenate(rows, axis=0)
    if is_own:
        side = int(math.isqrt(pairs))
        place = lax.broadcasted_iota(jnp.int32, got.shape, 1)
        got = jnp.where(place // side == place % side, 0.0, got)
    return got


def kernel(sta_count, offs, parts_ref, bins_ref, cells_ref, coarse_ref, fine_ref, out_ref,
           near, far, all_bins, all_cells, table, accs, picks, peer_picks, spread, landed, edge_own, edges,
           lhs, block_send, block_recv, index_send, index_recv, pick_sems, send_sem, recv_sem, edge_send, edge_recv):
    sta = lax.axis_index("sta")
    per = lax.axis_index("per")
    count = parts_ref.shape[1]
    pairs = count * count
    barrier = pltpu.get_barrier_semaphore()
    pl.semaphore_signal(barrier, inc=1, device_id=(sta, 1 - per), device_id_type=MESH)

    def greet(step, carry):
        there = lax.rem(sta + step, sta_count)
        pl.semaphore_signal(barrier, inc=1, device_id=(there, per), device_id_type=MESH)
        return carry

    lax.fori_loop(1, sta_count, greet, 0)

    build_table(coarse_ref, fine_ref, table, per)
    correlate_into([accs.at[0]], parts_ref, [parts_ref], table, CHUNK)

    pl.semaphore_wait(barrier, sta_count)

    def sent(src, dst, send, recv, there, half):
        copy = pltpu.make_async_remote_copy(
            src_ref=src, dst_ref=dst, send_sem=send, recv_sem=recv, device_id=(there, half), device_id_type=MESH)
        copy.start()
        return copy

    near_copy = sent(parts_ref, near, block_send.at[0], block_recv.at[0], lax.rem(sta + 1, sta_count), per)
    bins_copy = sent(bins_ref, all_bins.at[per], index_send.at[0], index_recv.at[0], sta, 1 - per)
    cells_copy = sent(cells_ref, all_cells.at[per], index_send.at[1], index_recv.at[1], sta, 1 - per)
    far_copy = sent(parts_ref, far, block_send.at[1], block_recv.at[1], lax.rem(sta + 2, sta_count), per)
    all_bins[per] = bins_ref[...]
    all_cells[per] = cells_ref[...]
    bins_copy.wait()
    cells_copy.wait()

    halves, residents = all_bins.shape[0], all_bins.shape[2]
    bins, cells = [], []
    for k in range(offs):
        cols = slice(k * count, (k + 1) * count)
        where = [(h, i) for h in range(halves) for i in range(residents)]
        bins.append(jnp.concatenate([all_bins[h, :, i, cols] for h, i in where], axis=1))
        cells.append(jnp.concatenate([all_cells[h, i, :, cols] for h, i in where], axis=1))
    cell = jnp.concatenate(cells, axis=1)
    ends = cell.shape[1]
    col = cell % 128
    row = cell // 128
    row = jnp.concatenate([row[0:1], row[1:2]], axis=1)
    col = jnp.concatenate([col[0:1], col[1:2]], axis=1)
    col_hot = (lax.broadcasted_iota(jnp.int32, (128, 2 * ends), 0) == col).astype(jnp.bfloat16)

    half = picks.shape[1]

    def pick(k):
        got = take_picks(accs[k], bins[k], k == 0)
        picks[0, :, k * pairs:(k + 1) * pairs] = got[:half]
        picks[1, :, k * pairs:(k + 1) * pairs] = got[half:]

    pick(0)
    near_copy.wait()
    correlate_into([accs.at[1]], parts_ref, [near], table, CHUNK)
    pick(1)
    far_copy.wait()
    correlate_into([accs.at[2]], parts_ref, [far], table, CHUNK)
    pick(2)

    trade = sent(picks.at[1 - per], peer_picks, pick_sems.at[0], pick_sems.at[1], sta, 1 - per)
    trade.wait()
    total = picks[per] + peer_picks[...]
    both = jnp.concatenate([total, total * total], axis=0)
    rows = both.shape[0]
    high = both.astype(jnp.bfloat16).astype(jnp.float32)
    low = both - high
    vals = jnp.concatenate([high, low], axis=0)
    vals = jnp.concatenate([vals, vals], axis=1)
    row = jnp.broadcast_to(row, vals.shape)

    group = 16
    for first in range(0, sta_count, group):
        for r in range(group):
            wanted = lax.rem(sta + (first + r), sta_count)
            lhs[r * 2 * rows:(r + 1) * 2 * rows, :] = jnp.where(row == wanted, vals, 0.0).astype(jnp.bfloat16)
        grid = lax.dot_general(lhs[...], col_hot, (((1,), (1,)), ((), ())), preferred_element_type=jnp.float32)
        grid = grid.reshape(group, 2, rows, 128)
        spread[first:first + group] = grid[:, 0] + grid[:, 1]

        def send(step, carry):
            sent(spread.at[step], landed.at[step - 1], send_sem, recv_sem, lax.rem(sta + step, sta_count), per)
            return carry

        lax.fori_loop(max(first, 1), first + group, send, 0)

    pltpu.make_async_copy(landed, landed, recv_sem).wait()
    edge_own[...] = spread[0] + jnp.sum(landed[...], axis=0)
    copies = [sent(edge_own, edges.at[side], edge_send.at[side], edge_recv.at[side], lax.rem(sta + step, sta_count), per)
              for side, step in enumerate((1, sta_count - 1))]
    own = edge_own[...]
    half = own.shape[0] // 2
    lane = lax.broadcasted_iota(jnp.int32, own.shape, 1)
    before_col = jnp.where(lane == 0, 0.0, pltpu.roll(own, 1, 1))
    after_col = jnp.where(lane == 127, 0.0, pltpu.roll(own, 127, 1))
    for copy in copies:
        copy.wait()
    before = jnp.where(sta == 0, 0.0, edges[0])
    after = jnp.where(sta == sta_count - 1, 0.0, edges[1])
    grad_rows = (after[:half] - before[:half]) * 0.5
    grad_cols = (after_col[:half] - before_col[:half]) * 0.5
    amp = 1.0 + own[half:]
    laplace = ((1.0 + after[half:]) + (1.0 + before[half:]) + (1.0 + after_col[half:])
               + (1.0 + before_col[half:]) - 4.0 * amp)
    period = per * half + lax.broadcasted_iota(jnp.int32, laplace.shape, 0)
    weight = 1.0 / (1.0 + period.astype(jnp.float32))
    result = grad_rows * grad_rows + grad_cols * grad_cols - weight * laplace / amp
    out_ref[...] = result[:, None, :]
    pltpu.make_async_copy(landed, landed, send_sem).wait()


def on_device(spectra, pick_bins, path_cells):
    per_count = lax.axis_size("per")
    sta_count = lax.axis_size("sta")
    count, _, band = spectra.shape
    pairs = count * count
    periods = pick_bins.shape[0]
    offs = pick_bins.shape[2] // count
    parts = jnp.transpose(spectra, (1, 0, 2))
    coarse, fine = angle_tables(per_count)
    local = periods // per_count
    rows = 2 * local
    vmem = pl.BlockSpec(memory_space=pltpu.VMEM)
    dma = pltpu.SemaphoreType.DMA
    return pl.pallas_call(
        functools.partial(kernel, sta_count, offs),
        out_shape=jax.ShapeDtypeStruct((local, 1, 128), jnp.float32),
        in_specs=[vmem] * 5,
        out_specs=vmem,
        scratch_shapes=[
            pltpu.VMEM(parts.shape, parts.dtype),
            pltpu.VMEM(parts.shape, parts.dtype),
            pltpu.VMEM((per_count,) + pick_bins.shape, jnp.int32),
            pltpu.VMEM((per_count,) + path_cells.shape, jnp.int32),
            pltpu.VMEM((2, band, NLAG), jnp.bfloat16),
            pltpu.VMEM((offs, pairs, NLAG), jnp.float32),
            pltpu.VMEM((per_count, local, offs * pairs), jnp.float32),
            pltpu.VMEM((local, offs * pairs), jnp.float32),
            pltpu.VMEM((sta_count, rows, 128), jnp.float32),
            pltpu.VMEM((sta_count - 1, rows, 128), jnp.float32),
            pltpu.VMEM((rows, 128), jnp.float32),
            pltpu.VMEM((2, rows, 128), jnp.float32),
            pltpu.VMEM((16 * 2 * rows, 2 * offs * pairs), jnp.bfloat16),
            dma((2,)), dma((2,)), dma((2,)), dma((2,)), dma((2,)), dma, dma, dma((2,)), dma((2,)),
        ],
        compiler_params=pltpu.CompilerParams(collective_id=0, has_side_effects=True),
        name="noise_map",
    )(parts, pick_bins, path_cells, coarse, fine)


def solution(mesh):
    return jax.shard_map(
        on_device,
        mesh=mesh,
        in_specs=(
            P("sta", None, "per"),
            P(None, ("sta", "per"), None),
            P(("sta", "per"), None, None),
        ),
        out_specs=P("per", "sta", None),
        check_vma=False,
    )
```

time: 50.6 us -> 45.5 us (0.90)
  starting transfers between devices: 6.16 us -> 0 us
  Pallas kernels: 36.4 us -> 42.3 us
  waiting for transfers between devices: 2.88 us -> 0 us
  local copies, waits for them, and re-layouts: 4.75 us -> 3.03 us
    ppermute x4 -> x0, starting transfers between devices: 6.16 us -> none  [the longest x2 4.13 us: along(): lax.ppermute(value, 'sta', [(i, (i + by) % sta_count) for i in range(sta_...]
    pallas_call x3 -> x1, Pallas kernels: 36.4 us -> 42.3 us  [on_device(): pl.pallas_call(functools.partial(kernel, sta_count, offs), out_shape=jax....]
    ppermute x4 -> x0, waiting for transfers between devices: 2.88 us -> none  [the longest x1 1.77 us: on_device(): cells_other = lax.ppermute(path_cells, 'per', swap)]
    reshape x4 -> x0, local copies, waits for them, and re-layouts: 1.63 us -> none  [the longest x1 0.72 us: on_device(): jnp.transpose(bins.reshape(periods, count, offs, count), (0, 2, 1, 3))]
    unnamed x12 -> x2, local copies, waits for them, and re-layouts: 3.1 us -> 3.03 us
  transfers between devices with their start and end apart: 4 -> 0, of which waited for: 2 -> 0; matrix products, arithmetic and copies ran while one was open for 3% -> 0% of each run, Pallas kernels for 10% -> 0%
where the time goes in v2:
time: 45.5 us; the launch traced here: 45.3 us
  Pallas kernels  42.3 us (93%)
  local copies, waits for them, and re-layouts  3.03 us (7%)
    pallas_call x1, Pallas kernels, on_device(): pl.pallas_call(functools.partial(kernel, sta_count, offs), out_shape=jax....  42.3 us
    unnamed x2, local copies, waits for them, and re-layouts  3.03 us

profile of v2, /device:TPU:0, one launch (start us, length us, event | category | flops | bytes accessed | tf_op | source)
XLA Modules:
  0.0 45.3 jit_solution(9564354168616493375)
XLA Ops:
  0.0 1.8 %copy.8 = bf16[16,2,4096]{2,0,1:T(8,128)(2,1)} copy(bf16[16,2,4096]{2,1,0:T(2,128)(2,1)} %param.5) | data formatting | bytes 524288 | tf_op args[0]
  1.8 42.3 %noise_map.1 = f32[4,1,128]{2,1,0:T(1,128)} custom-call(bf16[2,16,4096]{2,1,0:T(8,128)(2,1)} %bitcast.3, s32[8,8,48]{2,1,0:T(8,128)} %bins_ref.1, s32[8,2,48]{2,1,0:T(2,128)} %cells_ref.1, f32[2,2,32,128]{3,2,1,0:T(8,128)} %constant.4.clone.coarse_ref, f32[2,128,128]{2,1,0:T(8,128)} %constant.5.clone.fine_ref), custom_call_target="tpu_custom_call" | custom-call | tf_op jit(solution)/shard_map/noise_map/pallas_call | solution.py:226
  44.1 1.2 %copy.10 = f32[4,1,128]{2,1,0:T(1,128)} copy(f32[4,1,128]{2,1,0:T(1,128)} %noise_map.1) | data formatting | bytes 4096

commit v3 on v2

v3 whole, which is shorter than its diff:
```python
import functools
import math

import jax
import jax.numpy as jnp
import numpy as np
from jax import lax
from jax.experimental import pallas as pl
from jax.experimental.pallas import tpu as pltpu
from jax.sharding import PartitionSpec as P

FREQ = 8192
NLAG = 128
COARSE = 128
CHUNK = 512
PIECES = 2
GROUP = 16
MESH = pl.DeviceIdType.MESH


def angle_tables(per_count):
    lag = np.arange(NLAG, dtype=np.int64) - NLAG // 2
    coarse = np.arange(FREQ // COARSE, dtype=np.int64) * COARSE
    fine = np.arange(COARSE, dtype=np.int64)
    out = []
    for bins, scale in ((coarse, FREQ ** -0.5), (fine, 1.0)):
        turned = (bins[:, None] * lag[None, :]) % (2 * FREQ)
        phase = turned.astype(np.float64) * (math.pi / FREQ)
        out.append(np.stack([np.cos(phase), np.sin(phase)]).astype(np.float32) * np.float32(scale))
    coarse_table, fine_table = out
    coarse_table = coarse_table.reshape(2, per_count, -1, NLAG).transpose(1, 0, 2, 3)
    return coarse_table, fine_table


def build_table(coarse_ref, fine_ref, table_ref, per_place):
    band = table_ref.shape[1]

    def one(step, carry):
        c = coarse_ref[per_place, 0, pl.ds(step, 1), :]
        s = coarse_ref[per_place, 1, pl.ds(step, 1), :]
        rows = pl.ds(pl.multiple_of(step * COARSE, COARSE), COARSE)
        fc = fine_ref[0]
        fs = fine_ref[1]
        table_ref[0, rows, :] = (c * fc - s * fs).astype(jnp.bfloat16)
        table_ref[1, rows, :] = (-(s * fc + c * fs)).astype(jnp.bfloat16)
        return carry

    lax.fori_loop(0, band // COARSE, one, 0)


def correlate_into(acc, resident, visiting, table_ref, start, stop):
    count = resident.shape[1]
    if start == 0:
        acc[...] = jnp.zeros_like(acc)

    def one(step, carry):
        cols = pl.ds(pl.multiple_of(step * CHUNK, CHUNK), CHUNK)
        rre = resident[0, :, cols].astype(jnp.float32)
        rim = resident[1, :, cols].astype(jnp.float32)
        vre = visiting[0, :, cols].astype(jnp.float32)
        vim = visiting[1, :, cols].astype(jnp.float32)
        real, imag = [], []
        for i in range(count):
            a = rre[i:i + 1]
            b = rim[i:i + 1]
            real.append((a * vre + b * vim).astype(jnp.bfloat16))
            imag.append((b * vre - a * vim).astype(jnp.bfloat16))
        real = jnp.concatenate(real, axis=0)
        imag = jnp.concatenate(imag, axis=0)
        acc[...] += jnp.dot(real, table_ref[0, cols, :], preferred_element_type=jnp.float32) + jnp.dot(
            imag, table_ref[1, cols, :], preferred_element_type=jnp.float32
        )
        return carry

    lax.fori_loop(start // CHUNK, stop // CHUNK, one, 0)


def take_picks(acc, bins, is_own):
    turned = acc.T
    periods, pairs = bins.shape
    lag = lax.broadcasted_iota(jnp.int32, turned.shape, 0)
    rows = []
    for p in range(periods):
        rows.append(jnp.sum(jnp.where(lag == bins[p:p + 1], turned, 0.0), axis=0, keepdims=True))
    got = jnp.concatenate(rows, axis=0)
    if is_own:
        side = int(math.isqrt(pairs))
        place = lax.broadcasted_iota(jnp.int32, got.shape, 1)
        got = jnp.where(place // side == place % side, 0.0, got)
    return got


def kernel(sta_count, offs, parts_ref, bins_ref, cells_ref, coarse_ref, fine_ref, out_ref,
           blocks, all_bins, all_cells, table, accs, picks, peer_picks, spread, landed, edge_own, edges, lhs_first, lhs,
           own_sem, near_send, near_recv, far_send, far_recv, index_send, index_recv, row_sem, col_sem,
           pick_send, pick_recv, send_sem, recv_sem, edge_send, edge_recv):
    sta = lax.axis_index("sta")
    per = lax.axis_index("per")
    even = lax.rem(sta, 2) == 0
    count = blocks.shape[2]
    band = blocks.shape[3]
    pairs = count * count
    piece = band // PIECES

    def around(step):
        return lax.rem(sta + (step + sta_count), sta_count)

    def digit_peers(stride):
        place = lax.rem(sta // stride, 4)
        return [sta + stride * (lax.rem(place + step, 4) - place) for step in (1, 2, 3)]

    def signal(sem, there, half):
        pl.semaphore_signal(sem, inc=1, device_id=(there, half), device_id_type=MESH)

    barrier = pltpu.get_barrier_semaphore()
    signal(barrier, sta, 1 - per)
    for step in (1, -1, 2, -2):
        signal(barrier, around(step), per)
    for step in (2, -2):
        signal(barrier, around(step), 1 - per)
    for stride in (1, 4, 16):
        for there in digit_peers(stride):
            signal(barrier, there, per)

    own = pltpu.make_async_copy(parts_ref, blocks.at[0], own_sem)
    own.start()
    build_table(coarse_ref, fine_ref, table, per)
    own.wait()
    pl.semaphore_wait(barrier, 16)

    def copy(src, dst, send, recv, there, half):
        return pltpu.make_async_remote_copy(
            src_ref=src, dst_ref=dst, send_sem=send, recv_sem=recv, device_id=(there, half), device_id_type=MESH)

    def index_copies(there, half, slot, sems):
        return [copy(bins_ref, all_bins.at[slot, per], index_send.at[sems, 0], index_recv.at[slot, per, 0], there, half),
                copy(cells_ref, all_cells.at[slot, per], index_send.at[sems, 1], index_recv.at[slot, per, 1], there, half)]

    def cut(slot, number):
        return blocks.at[slot, :, :, pl.ds(number * piece, piece)]

    for c in index_copies(sta, 1 - per, 0, 0):
        c.start()
    near = [copy(cut(0, n), cut(1, n), near_send.at[n], near_recv.at[n], around(1), per) for n in range(PIECES)]
    back = [copy(cut(0, n), cut(2, n), far_send.at[0, n], far_recv.at[n], around(-2), per) for n in range(PIECES)]
    along = [copy(cut(1, n), cut(2, n), far_send.at[1, n], far_recv.at[n], around(1), per) for n in range(PIECES)]
    for n in range(PIECES):
        near[n].start()

        @pl.when(even)
        def _():
            back[n].start()

    @pl.when(even)
    def _():
        for half, sems in ((per, 1), (1 - per, 2)):
            for c in index_copies(around(-2), half, 1, sems):
                c.start()

    for there in digit_peers(16):
        signal(row_sem, there, per)

    correlate_into(accs.at[0], blocks.at[0], blocks.at[0], table, 0, band)

    pl.semaphore_wait(row_sem, 3)
    for there in digit_peers(4):
        signal(col_sem, there, per)

    all_bins[0, per] = bins_ref[...]
    all_cells[0, per] = cells_ref[...]
    for ref, kind in ((bins_ref, 0), (cells_ref, 1)):
        pltpu.make_async_copy(ref, ref, index_recv.at[0, 1 - per, kind]).wait()
        pltpu.make_async_copy(ref, ref, index_send.at[0, kind]).wait()

    @pl.when(even)
    def _():
        for half in range(2):
            for ref, kind in ((bins_ref, 0), (cells_ref, 1)):
                pltpu.make_async_copy(ref, ref, index_recv.at[1, half, kind]).wait()
                pltpu.make_async_copy(ref, ref, index_send.at[1 + half, kind]).wait()

    far_set = jnp.where(even, 1, 0)
    halves, residents = all_bins.shape[1], all_bins.shape[3]
    spots = [(h, i) for h in range(halves) for i in range(residents)]

    def bins_of(k):
        cols = slice(k * count, (k + 1) * count)
        which = far_set if k == offs - 1 else 0
        return jnp.concatenate([all_bins[which, h, :, i, cols] for h, i in spots], axis=1)

    def cells_of(k):
        cols = slice(k * count, (k + 1) * count)
        which = far_set if k == offs - 1 else 0
        return jnp.concatenate([all_cells[which, h, i, :, cols] for h, i in spots], axis=1)

    half = picks.shape[1]

    def pick(k):
        got = take_picks(accs[k], bins_of(k), k == 0)
        picks[0, :, k * pairs:(k + 1) * pairs] = got[:half]
        picks[1, :, k * pairs:(k + 1) * pairs] = got[half:]

    pick(0)
    for n in range(PIECES):
        near[n].wait_recv()

        @pl.when(even)
        def _():
            along[n].start()

        correlate_into(accs.at[1], blocks.at[0], blocks.at[1], table, n * piece, (n + 1) * piece)
    pick(1)

    def trade(number, start, stop):
        lanes = pl.ds(start, stop - start)
        return copy(picks.at[1 - per, :, lanes], peer_picks.at[:, lanes], pick_send.at[number], pick_recv.at[number],
                    sta, 1 - per)

    split = (offs - 1) * pairs
    first_trade = trade(0, 0, split)
    first_trade.start()
    resident = blocks.at[jnp.where(even, 2, 0)]
    visiting = blocks.at[jnp.where(even, 0, 2)]
    for n in range(PIECES):
        back[n].wait_recv()
        correlate_into(accs.at[2], resident, visiting, table, n * piece, (n + 1) * piece)
    pick(2)
    last_trade = trade(1, split, offs * pairs)
    last_trade.start()
    pl.semaphore_wait(col_sem, 3)

    rows = 2 * half

    def ends_of(ks):
        cell = jnp.concatenate([cells_of(k) for k in ks], axis=1)
        row = cell // 128
        col = cell % 128
        row = jnp.concatenate([row[0:1], row[1:2]], axis=1)
        col = jnp.concatenate([col[0:1], col[1:2]], axis=1)
        hot = (lax.broadcasted_iota(jnp.int32, (128, col.shape[1]), 0) == col).astype(jnp.bfloat16)
        return jnp.broadcast_to(row, (2 * rows, row.shape[1])), hot

    def values(start, stop):
        total = picks[per, :, start:stop] + peer_picks[:, start:stop]
        both = jnp.concatenate([total, total * total], axis=0)
        high = both.astype(jnp.bfloat16).astype(jnp.float32)
        vals = jnp.concatenate([high, both - high], axis=0)
        return jnp.concatenate([vals, vals], axis=1)

    def add_up(lhs_ref, first, group, row, vals, hot):
        for r in range(group):
            wanted = around(first + r)
            lhs_ref[r * 2 * rows:(r + 1) * 2 * rows, :] = jnp.where(row == wanted, vals, 0.0).astype(jnp.bfloat16)
        grid = lax.dot_general(lhs_ref[...], hot, (((1,), (1,)), ((), ())), preferred_element_type=jnp.float32)
        grid = grid.reshape(group, 2, rows, 128)
        return grid[:, 0] + grid[:, 1]

    row, hot = ends_of(range(offs - 1))
    first_trade.wait()
    vals = values(0, split)
    for first in range(0, sta_count, GROUP):
        spread[first:first + GROUP] = add_up(lhs_first, first, GROUP, row, vals, hot)
    row, hot = ends_of([offs - 1])
    last_trade.wait()
    vals = values(split, offs * pairs)
    for first in range(0, sta_count, GROUP):
        spread[first:first + GROUP] += add_up(lhs, first, GROUP, row, vals, hot)

        def send(step, carry):
            copy(spread.at[step], landed.at[step - 1], send_sem, recv_sem, around(step), per).start()
            return carry

        lax.fori_loop(max(first, 1), first + GROUP, send, 0)

    for n in range(PIECES):
        near[n].wait_send()

        @pl.when(even)
        def _():
            back[n].wait_send()
            along[n].wait_send()

    pltpu.make_async_copy(landed, landed, recv_sem).wait()
    edge_own[...] = spread[0] + jnp.sum(landed[...], axis=0)
    sides = [copy(edge_own, edges.at[side], edge_send.at[side], edge_recv.at[side], around(step), per)
             for side, step in enumerate((1, -1))]
    for c in sides:
        c.start()
    mine = edge_own[...]
    lane = lax.broadcasted_iota(jnp.int32, mine.shape, 1)
    before_col = jnp.where(lane == 0, 0.0, pltpu.roll(mine, 1, 1))
    after_col = jnp.where(lane == 127, 0.0, pltpu.roll(mine, 127, 1))
    for c in sides:
        c.wait()
    before = jnp.where(sta == 0, 0.0, edges[0])
    after = jnp.where(sta == sta_count - 1, 0.0, edges[1])
    grad_rows = (after[:half] - before[:half]) * 0.5
    grad_cols = (after_col[:half] - before_col[:half]) * 0.5
    amp = 1.0 + mine[half:]
    laplace = ((1.0 + after[half:]) + (1.0 + before[half:]) + (1.0 + after_col[half:])
               + (1.0 + before_col[half:]) - 4.0 * amp)
    period = per * half + lax.broadcasted_iota(jnp.int32, laplace.shape, 0)
    weight = 1.0 / (1.0 + period.astype(jnp.float32))
    result = grad_rows * grad_rows + grad_cols * grad_cols - weight * laplace / amp
    out_ref[...] = result[:, None, :]
    pltpu.make_async_copy(landed, landed, send_sem).wait()


def on_device(spectra, pick_bins, path_cells):
    per_count = lax.axis_size("per")
    sta_count = lax.axis_size("sta")
    count, _, band = spectra.shape
    pairs = count * count
    periods = pick_bins.shape[0]
    offs = pick_bins.shape[2] // count
    parts = jnp.transpose(spectra, (1, 0, 2))
    coarse, fine = angle_tables(per_count)
    local = periods // per_count
    rows = 2 * local
    vmem = pl.BlockSpec(memory_space=pltpu.VMEM)
    dma = pltpu.SemaphoreType.DMA
    regular = pltpu.SemaphoreType.REGULAR
    return pl.pallas_call(
        functools.partial(kernel, sta_count, offs),
        out_shape=jax.ShapeDtypeStruct((local, 1, 128), jnp.float32),
        in_specs=[pl.BlockSpec(memory_space=pl.ANY)] + [vmem] * 4,
        out_specs=vmem,
        scratch_shapes=[
            pltpu.VMEM((3,) + parts.shape, parts.dtype),
            pltpu.VMEM((2, per_count) + pick_bins.shape, jnp.int32),
            pltpu.VMEM((2, per_count) + path_cells.shape, jnp.int32),
            pltpu.VMEM((2, band, NLAG), jnp.bfloat16),
            pltpu.VMEM((offs, pairs, NLAG), jnp.float32),
            pltpu.VMEM((per_count, local, offs * pairs), jnp.float32),
            pltpu.VMEM((local, offs * pairs), jnp.float32),
            pltpu.VMEM((sta_count, rows, 128), jnp.float32),
            pltpu.VMEM((sta_count - 1, rows, 128), jnp.float32),
            pltpu.VMEM((rows, 128), jnp.float32),
            pltpu.VMEM((2, rows, 128), jnp.float32),
            pltpu.VMEM((GROUP * 2 * rows, 2 * (offs - 1) * pairs), jnp.bfloat16),
            pltpu.VMEM((GROUP * 2 * rows, 2 * pairs), jnp.bfloat16),
            dma, dma((PIECES,)), dma((PIECES,)), dma((2, PIECES)), dma((PIECES,)), dma((3, 2)), dma((2, 2, 2)),
            regular, regular, dma((2,)), dma((2,)), dma, dma, dma((2,)), dma((2,)),
        ],
        compiler_params=pltpu.CompilerParams(collective_id=0, has_side_effects=True),
        name="noise_map",
    )(parts, pick_bins, path_cells, coarse, fine)


def solution(mesh):
    return jax.shard_map(
        on_device,
        mesh=mesh,
        in_specs=(
            P("sta", None, "per"),
            P(None, ("sta", "per"), None),
            P(("sta", "per"), None, None),
        ),
        out_specs=P("per", "sta", None),
        check_vma=False,
    )
```

time: 45.5 us -> 42.4 us (0.932)
  Pallas kernels: 42.3 us -> 39.2 us
    pallas_call x1, Pallas kernels: 42.3 us -> 39.2 us  [on_device(): pl.pallas_call(functools.partial(kernel, sta_count, offs), out_shape=jax....]
where the time goes in v3:
time: 42.4 us; the launch traced here: 42.2 us
  Pallas kernels  39.2 us (92%)
  local copies, waits for them, and re-layouts  3.03 us (7%)
    pallas_call x1, Pallas kernels, on_device(): pl.pallas_call(functools.partial(kernel, sta_count, offs), out_shape=jax....  39.2 us
    unnamed x2, local copies, waits for them, and re-layouts  3.03 us

profile of v3, /device:TPU:0, one launch (start us, length us, event | category | flops | bytes accessed | tf_op | source)
XLA Modules:
  0.0 42.2 jit_solution(9764157495338597285)
XLA Ops:
  0.0 1.8 %copy.8 = bf16[16,2,4096]{2,0,1:T(8,128)(2,1)} copy(bf16[16,2,4096]{2,1,0:T(2,128)(2,1)} %param.5) | data formatting | bytes 524288 | tf_op args[0]
  1.8 39.2 %noise_map.1 = f32[4,1,128]{2,1,0:T(1,128)} custom-call(bf16[2,16,4096]{2,1,0:T(8,128)(2,1)} %bitcast.3, s32[8,8,48]{2,1,0:T(8,128)} %bins_ref.1, s32[8,2,48]{2,1,0:T(2,128)} %cells_ref.1, f32[2,2,32,128]{3,2,1,0:T(8,128)} %constant.4.clone.coarse_ref, f32[2,128,128]{2,1,0:T(8,128)} %constant.5.clone.fine_ref), custom_call_target="tpu_custom_call" | custom-call | tf_op jit(solution)/shard_map/noise_map/pallas_call | solution.py:323
  41.0 1.2 %copy.10 = f32[4,1,128]{2,1,0:T(1,128)} copy(f32[4,1,128]{2,1,0:T(1,128)} %noise_map.1) | data formatting | bytes 4096

commit v4 on v3

--- a/solution.py
+++ b/solution.py
@@ -124,7 +124,6 @@
 
     own = pltpu.make_async_copy(parts_ref, blocks.at[0], own_sem)
     own.start()
-    build_table(coarse_ref, fine_ref, table, per)
     own.wait()
     pl.semaphore_wait(barrier, 16)
 
@@ -160,6 +159,7 @@
     for there in digit_peers(16):
         signal(row_sem, there, per)
 
+    build_table(coarse_ref, fine_ref, table, per)
     correlate_into(accs.at[0], blocks.at[0], blocks.at[0], table, 0, band)
 
     pl.semaphore_wait(row_sem, 3)
@@ -171,13 +171,6 @@
     for ref, kind in ((bins_ref, 0), (cells_ref, 1)):
         pltpu.make_async_copy(ref, ref, index_recv.at[0, 1 - per, kind]).wait()
         pltpu.make_async_copy(ref, ref, index_send.at[0, kind]).wait()
-
-    @pl.when(even)
-    def _():
-        for half in range(2):
-            for ref, kind in ((bins_ref, 0), (cells_ref, 1)):
-                pltpu.make_async_copy(ref, ref, index_recv.at[1, half, kind]).wait()
-                pltpu.make_async_copy(ref, ref, index_send.at[1 + half, kind]).wait()
 
     far_set = jnp.where(even, 1, 0)
     halves, residents = all_bins.shape[1], all_bins.shape[3]
@@ -224,6 +217,14 @@
     for n in range(PIECES):
         back[n].wait_recv()
         correlate_into(accs.at[2], resident, visiting, table, n * piece, (n + 1) * piece)
+
+    @pl.when(even)
+    def _():
+        for half in range(2):
+            for ref, kind in ((bins_ref, 0), (cells_ref, 1)):
+                pltpu.make_async_copy(ref, ref, index_recv.at[1, half, kind]).wait()
+                pltpu.make_async_copy(ref, ref, index_send.at[1 + half, kind]).wait()
+
     pick(2)
     last_trade = trade(1, split, offs * pairs)
     last_trade.start()

time: 42.4 us -> 40.2 us (0.948)
  Pallas kernels: 39.2 us -> 37 us
    pallas_call x1, Pallas kernels: 39.2 us -> 37 us  [on_device(): pl.pallas_call(functools.partial(kernel, sta_count, offs), out_shape=jax....]
where the time goes in v4:
time: 40.2 us; the launch traced here: 40 us
  Pallas kernels  37 us (92%)
  local copies, waits for them, and re-layouts  3.03 us (8%)
    pallas_call x1, Pallas kernels, on_device(): pl.pallas_call(functools.partial(kernel, sta_count, offs), out_shape=jax....  37 us
    unnamed x2, local copies, waits for them, and re-layouts  3.03 us

profile of v4, /device:TPU:0, one launch (start us, length us, event | category | flops | bytes accessed | tf_op | source)
XLA Modules:
  0.0 40.0 jit_solution(9901320373100207568)
XLA Ops:
  0.0 1.8 %copy.8 = bf16[16,2,4096]{2,0,1:T(8,128)(2,1)} copy(bf16[16,2,4096]{2,1,0:T(2,128)(2,1)} %param.5) | data formatting | bytes 524288 | tf_op args[0]
  1.8 37.0 %noise_map.1 = f32[4,1,128]{2,1,0:T(1,128)} custom-call(bf16[2,16,4096]{2,1,0:T(8,128)(2,1)} %bitcast.3, s32[8,8,48]{2,1,0:T(8,128)} %bins_ref.1, s32[8,2,48]{2,1,0:T(2,128)} %cells_ref.1, f32[2,2,32,128]{3,2,1,0:T(8,128)} %constant.4.clone.coarse_ref, f32[2,128,128]{2,1,0:T(8,128)} %constant.5.clone.fine_ref), custom_call_target="tpu_custom_call" | custom-call | tf_op jit(solution)/shard_map/noise_map/pallas_call | solution.py:324
  38.8 1.2 %copy.10 = f32[4,1,128]{2,1,0:T(1,128)} copy(f32[4,1,128]{2,1,0:T(1,128)} %noise_map.1) | data formatting | bytes 4096

commit v5 on v4

--- a/solution.py
+++ b/solution.py
@@ -91,9 +91,9 @@
 
 
 def kernel(sta_count, offs, parts_ref, bins_ref, cells_ref, coarse_ref, fine_ref, out_ref,
-           blocks, all_bins, all_cells, table, accs, picks, peer_picks, spread, landed, edge_own, edges, lhs_first, lhs,
+           blocks, all_bins, all_cells, table, accs, picks, peer_picks, spread, chip_landed, landed, outer_landed, edge_own, edge_mate, lhs_first, lhs,
            own_sem, near_send, near_recv, far_send, far_recv, index_send, index_recv, row_sem, col_sem,
-           pick_send, pick_recv, send_sem, recv_sem, edge_send, edge_recv):
+           pick_send, pick_recv, chip_send, chip_recv, send_sem, recv_sem, outer_send, outer_recv, edge_send, edge_recv):
     sta = lax.axis_index("sta")
     per = lax.axis_index("per")
     even = lax.rem(sta, 2) == 0
@@ -248,9 +248,14 @@
         vals = jnp.concatenate([high, both - high], axis=0)
         return jnp.concatenate([vals, vals], axis=1)
 
-    def add_up(lhs_ref, first, group, row, vals, hot):
+    core = lax.rem(sta, 2)
+    mates = [sta + 1 - 2 * core, sta]
+    chips = sta_count // 2
+    groups = list(reversed(range(0, chips, GROUP)))
+
+    def add_up(lhs_ref, which, first, group, row, vals, hot):
         for r in range(group):
-            wanted = around(first + r)
+            wanted = lax.rem(mates[which] + 2 * (first + r), sta_count)
             lhs_ref[r * 2 * rows:(r + 1) * 2 * rows, :] = jnp.where(row == wanted, vals, 0.0).astype(jnp.bfloat16)
         grid = lax.dot_general(lhs_ref[...], hot, (((1,), (1,)), ((), ())), preferred_element_type=jnp.float32)
         grid = grid.reshape(group, 2, rows, 128)
@@ -259,19 +264,36 @@
     row, hot = ends_of(range(offs - 1))
     first_trade.wait()
     vals = values(0, split)
-    for first in range(0, sta_count, GROUP):
-        spread[first:first + GROUP] = add_up(lhs_first, first, GROUP, row, vals, hot)
+    for which in range(2):
+        for first in groups:
+            spread[which, first:first + GROUP] = add_up(lhs_first, which, first, GROUP, row, vals, hot)
     row, hot = ends_of([offs - 1])
     last_trade.wait()
     vals = values(split, offs * pairs)
-    for first in range(0, sta_count, GROUP):
-        spread[first:first + GROUP] += add_up(lhs, first, GROUP, row, vals, hot)
+    to_mate = []
+    for n, first in enumerate(groups):
+        spread[0, first:first + GROUP] += add_up(lhs, 0, first, GROUP, row, vals, hot)
+        span = pl.ds(first, GROUP)
+        to_mate.append(copy(spread.at[0, span], chip_landed.at[span], chip_send.at[n], chip_recv.at[n], mates[0], per))
+        to_mate[n].start()
+    for n, first in enumerate(groups):
+        part = add_up(lhs, 1, first, GROUP, row, vals, hot)
+        to_mate[n].wait_recv()
+        spread[1, first:first + GROUP] += part + chip_landed[first:first + GROUP]
+
+        def send_outer(step, carry):
+            there = around(2 * step + 2 * core - 1)
+            copy(spread.at[1, step], outer_landed.at[step], outer_send, outer_recv, there, per).start()
+            return carry
 
         def send(step, carry):
-            copy(spread.at[step], landed.at[step - 1], send_sem, recv_sem, around(step), per).start()
+            copy(spread.at[1, step], landed.at[step - 1], send_sem, recv_sem, around(2 * step), per).start()
             return carry
 
         lax.fori_loop(max(first, 1), first + GROUP, send, 0)
+        lax.fori_loop(first, first + GROUP, send_outer, 0)
+    for c in to_mate:
+        c.wait_send()
 
     for n in range(PIECES):
         near[n].wait_send()
@@ -282,19 +304,19 @@
             along[n].wait_send()
 
     pltpu.make_async_copy(landed, landed, recv_sem).wait()
-    edge_own[...] = spread[0] + jnp.sum(landed[...], axis=0)
-    sides = [copy(edge_own, edges.at[side], edge_send.at[side], edge_recv.at[side], around(step), per)
-             for side, step in enumerate((1, -1))]
-    for c in sides:
-        c.start()
+    edge_own[...] = spread[1, 0] + jnp.sum(landed[...], axis=0)
+    to_edge = copy(edge_own, edge_mate, edge_send, edge_recv, mates[0], per)
+    to_edge.start()
     mine = edge_own[...]
     lane = lax.broadcasted_iota(jnp.int32, mine.shape, 1)
     before_col = jnp.where(lane == 0, 0.0, pltpu.roll(mine, 1, 1))
     after_col = jnp.where(lane == 127, 0.0, pltpu.roll(mine, 127, 1))
-    for c in sides:
-        c.wait()
-    before = jnp.where(sta == 0, 0.0, edges[0])
-    after = jnp.where(sta == sta_count - 1, 0.0, edges[1])
+    pltpu.make_async_copy(outer_landed, outer_landed, outer_recv).wait()
+    outer = jnp.sum(outer_landed[...], axis=0)
+    to_edge.wait()
+    mate = edge_mate[...]
+    before = jnp.where(sta == 0, 0.0, jnp.where(even, outer, mate))
+    after = jnp.where(sta == sta_count - 1, 0.0, jnp.where(even, mate, outer))
     grad_rows = (after[:half] - before[:half]) * 0.5
     grad_cols = (after_col[:half] - before_col[:half]) * 0.5
     amp = 1.0 + mine[half:]
@@ -305,6 +327,7 @@
     result = grad_rows * grad_rows + grad_cols * grad_cols - weight * laplace / amp
     out_ref[...] = result[:, None, :]
     pltpu.make_async_copy(landed, landed, send_sem).wait()
+    pltpu.make_async_copy(outer_landed, outer_landed, outer_send).wait()
 
 
 def on_device(spectra, pick_bins, path_cells):
@@ -334,14 +357,16 @@
             pltpu.VMEM((offs, pairs, NLAG), jnp.float32),
             pltpu.VMEM((per_count, local, offs * pairs), jnp.float32),
             pltpu.VMEM((local, offs * pairs), jnp.float32),
-            pltpu.VMEM((sta_count, rows, 128), jnp.float32),
-            pltpu.VMEM((sta_count - 1, rows, 128), jnp.float32),
+            pltpu.VMEM((2, sta_count // 2, rows, 128), jnp.float32),
+            pltpu.VMEM((sta_count // 2, rows, 128), jnp.float32),
+            pltpu.VMEM((sta_count // 2 - 1, rows, 128), jnp.float32),
+            pltpu.VMEM((sta_count // 2, rows, 128), jnp.float32),
             pltpu.VMEM((rows, 128), jnp.float32),
-            pltpu.VMEM((2, rows, 128), jnp.float32),
+            pltpu.VMEM((rows, 128), jnp.float32),
             pltpu.VMEM((GROUP * 2 * rows, 2 * (offs - 1) * pairs), jnp.bfloat16),
             pltpu.VMEM((GROUP * 2 * rows, 2 * pairs), jnp.bfloat16),
             dma, dma((PIECES,)), dma((PIECES,)), dma((2, PIECES)), dma((PIECES,)), dma((3, 2)), dma((2, 2, 2)),
-            regular, regular, dma((2,)), dma((2,)), dma, dma, dma((2,)), dma((2,)),
+            regular, regular, dma((2,)), dma((2,)), dma((2,)), dma((2,)), dma, dma, dma, dma, dma, dma,
         ],
         compiler_params=pltpu.CompilerParams(collective_id=0, has_side_effects=True),
         name="noise_map",

time: 40.2 us -> 39.2 us (0.975)
  the two profiles are of different devices: /device:TPU:0 before, /device:TPU:1 now
where the time goes in v5:
time: 39.2 us; the launch traced here: 39 us
  Pallas kernels  36 us (92%)
  local copies, waits for them, and re-layouts  3.03 us (8%)
    pallas_call x1, Pallas kernels, on_device(): pl.pallas_call(functools.partial(kernel, sta_count, offs), out_shape=jax....  36 us
    unnamed x2, local copies, waits for them, and re-layouts  3.03 us

profile of v5, /device:TPU:1, one launch (start us, length us, event | category | flops | bytes accessed | tf_op | source)
XLA Modules:
  0.0 39.0 jit_solution(16224764405621761683)
XLA Ops:
  0.0 1.8 %copy.8 = bf16[16,2,4096]{2,0,1:T(8,128)(2,1)} copy(bf16[16,2,4096]{2,1,0:T(2,128)(2,1)} %param.5) | data formatting | bytes 524288 | tf_op args[0]
  1.8 36.0 %noise_map.1 = f32[4,1,128]{2,1,0:T(1,128)} custom-call(bf16[2,16,4096]{2,1,0:T(8,128)(2,1)} %bitcast.3, s32[8,8,48]{2,1,0:T(8,128)} %bins_ref.1, s32[8,2,48]{2,1,0:T(2,128)} %cells_ref.1, f32[2,2,32,128]{3,2,1,0:T(8,128)} %constant.4.clone.coarse_ref, f32[2,128,128]{2,1,0:T(8,128)} %constant.5.clone.fine_ref), custom_call_target="tpu_custom_call" | custom-call | tf_op jit(solution)/shard_map/noise_map/pallas_call | solution.py:347
  37.8 1.2 %copy.10 = f32[4,1,128]{2,1,0:T(1,128)} copy(f32[4,1,128]{2,1,0:T(1,128)} %noise_map.1) | data formatting | bytes 4096

commit v6 on v5

--- a/solution.py
+++ b/solution.py
@@ -12,7 +12,7 @@
 FREQ = 8192
 NLAG = 128
 COARSE = 128
-CHUNK = 512
+CHUNK = 1024
 PIECES = 2
 GROUP = 16
 MESH = pl.DeviceIdType.MESH

time: 39.2 us -> 38.4 us (0.980)
  Pallas kernels: 36 us -> 35.1 us
    pallas_call x1, Pallas kernels: 36 us -> 35.1 us  [on_device(): pl.pallas_call(functools.partial(kernel, sta_count, offs), out_shape=jax....]
where the time goes in v6:
time: 38.4 us; the launch traced here: 38.2 us
  Pallas kernels  35.1 us (91%)
  local copies, waits for them, and re-layouts  3.03 us (8%)
    pallas_call x1, Pallas kernels, on_device(): pl.pallas_call(functools.partial(kernel, sta_count, offs), out_shape=jax....  35.1 us
    unnamed x2, local copies, waits for them, and re-layouts  3.03 us

profile of v6, /device:TPU:1, one launch (start us, length us, event | category | flops | bytes accessed | tf_op | source)
XLA Modules:
  0.0 38.2 jit_solution(391376187082385916)
XLA Ops:
  0.0 1.8 %copy.8 = bf16[16,2,4096]{2,0,1:T(8,128)(2,1)} copy(bf16[16,2,4096]{2,1,0:T(2,128)(2,1)} %param.5) | data formatting | bytes 524288 | tf_op args[0]
  1.8 35.1 %noise_map.1 = f32[4,1,128]{2,1,0:T(1,128)} custom-call(bf16[2,16,4096]{2,1,0:T(8,128)(2,1)} %bitcast.3, s32[8,8,48]{2,1,0:T(8,128)} %bins_ref.1, s32[8,2,48]{2,1,0:T(2,128)} %cells_ref.1, f32[2,2,32,128]{3,2,1,0:T(8,128)} %constant.4.clone.coarse_ref, f32[2,128,128]{2,1,0:T(8,128)} %constant.5.clone.fine_ref), custom_call_target="tpu_custom_call" | custom-call | tf_op jit(solution)/shard_map/noise_map/pallas_call | solution.py:347
  36.9 1.2 %copy.10 = f32[4,1,128]{2,1,0:T(1,128)} copy(f32[4,1,128]{2,1,0:T(1,128)} %noise_map.1) | data formatting | bytes 4096
